TPU v7x, 32 devices: a whole 2x2x4 slice. The times are simulated.
32 devices in a mesh: groups: 2 (over x), row: 16 (over z, y, core).
Axes of the slice: x: 2, y: 2, z: 4, core: 2. Of those that a mesh axis runs over, the one named last changes fastest.
Arguments:
- inputs: bfloat16 [1024, 8192], P(('groups', 'row')), parts along dimension 0, may hold values from -6 to 6
- input_factor: bfloat16 [16384, 8192], P(('groups', 'row')), parts along dimension 0, as said below
- out_grads: bfloat16 [1024, 16384], P(('groups', 'row')), parts along dimension 0, may hold values from -6 to 6
- output_factor: float32 [32768, 4096], P(('groups', 'row')), parts along dimension 0, may hold values from -6 to 6
Outputs:
- updated_factor: float32 [32768, 4096], P(('groups', 'row')), parts along dimension 0
There are 2 independent parts, one for each index of `groups`. A program takes and returns all parts, laid end to end along the dimension named above; each array names one. Nothing has to cross between parts.
Inputs may be any that keep to these rules, and one draw needn't show every extreme that they name: input_factor is symmetric.
All inputs are finite; a program needn't handle non-finite values.
Results may differ from a plain program's by a relative error of at most 0.0041.
Values may be sent and summed in bfloat16 or wider, within the bound.
A program may use at most 192 MiB of HBM per device.

v0:
```python
import jax
import jax.numpy as jnp
from jax import lax
from jax.sharding import PartitionSpec as P


def per_device(inputs, input_factor, out_grads, output_factor):
    grad_cols = lax.all_to_all(out_grads, "row", split_axis=1, concat_axis=0, tiled=True)
    whole = lax.all_gather(inputs, "row", axis=0, tiled=True)
    proj_half = lax.dot_general(
        input_factor, whole, (((1,), (1,)), ((), ())), preferred_element_type=jnp.float32
    ).astype(jnp.bfloat16)
    feature_width = input_factor.shape[0]
    own_cols = lax.dynamic_slice_in_dim(
        whole, lax.axis_index("row") * feature_width, feature_width, 1
    )
    partial_value = lax.dot_general(
        proj_half, own_cols, (((0,), (1,)), ((), ())), preferred_element_type=jnp.float32
    )
    factor = float(input_factor.shape[1]) ** (-0.5)
    gram = (lax.psum(partial_value, "row") * factor).astype(jnp.bfloat16)
    left = lax.dot_general(
        grad_cols, gram, (((0,), (0,)), ((), ())), preferred_element_type=jnp.float32
    ).astype(jnp.bfloat16)
    slab_width = output_factor.shape[1]
    slab_all = lax.all_gather(out_grads[:, :slab_width], "row", axis=0, tiled=True)
    update = jnp.dot(left, slab_all, preferred_element_type=jnp.float32)
    return output_factor + update * (1.0 / gram.shape[0])


def solution(mesh):
    in_specs = (
        P(("groups", "row"), None),
        P(("groups", "row"), None),
        P(("groups", "row"), None),
        P(("groups", "row"), None),
    )
    out_specs = P(("groups", "row"), None)
    return jax.shard_map(
        per_device, mesh=mesh, in_specs=in_specs, out_specs=out_specs, check_vma=False
    )
```

profile of v0, /device:TPU:0, one launch (start us, length us, event | category | flops | bytes accessed | tf_op | source)
XLA Modules:
  0.0 273.1 jit_solution(11603541428070253687)
XLA Ops:
  6.5 0.0 all-gather.3.cloned.1.call-start
  6.5 0.7 all-gather.3.cloned.1.call-update
  7.3 0.0 all-gather.5.cloned.1.call-start
  7.3 1.7 slice.3
  9.0 0.0 all-gather.5.cloned.1.call-update
  9.0 2.3 copy.9
  11.3 7.4 %all-to-all-start = ((bf16[32,16,1024]{2,0,1:T(8,128)(2,1)}), bf16[32,16,1024]{2,0,1:T(8,128)(2,1)S(1)}, u32[]{:S(2)}, u32[]{:S(2)}) async-start(bf16[32,16,1024]{2,0,1:T(8,128)(2,1)} %bitcast.10), calls=%async_computation | async-start | bytes 2097152 | tf_op jit(solution)/shard_map/all_to_all | solution.py:8
  18.7 0.0 all-reduce.2.cloned.1.call-start
  18.8 87.2 %all-gather.3.cloned.1.call-done = bf16[512,8192]{1,0:T(8,128)(2,1)} async-done(((bf16[32,8192]{1,0:T(8,128)(2,1)}), bf16[512,8192]{1,0:T(8,128)(2,1)}) %all-gather.3.cloned.1.call-update) | async-done | bytes 8388624 | tf_op jit(solution)/shard_map/all_gather | solution.py:9
  105.9 11.8 %fusion = f32[512,512]{1,0:T(8,128)} fusion(bf16[512,8192]{1,0:T(8,128)(2,1)} %param.5, bf16[512,8192]{1,0:T(8,128)(2,1)} %all-gather.3.cloned.1.call-done, s32[]{:T(128)S(6)} %select_n.3), kind=kOutput, calls=%fused_computation.3 | convolution fusion | flops 4563664896 | bytes 18350084 | tf_op jit(solution)/shard_map/dot_general | solution.py:17
  117.7 0.0 all-reduce.2.cloned.1.call-update
  117.7 0.0 all-to-all-done
  117.7 39.4 %all-gather.5.cloned.1.call-done = bf16[512,4096]{1,0:T(8,128)(2,1)} async-done(((bf16[32,4096]{1,0:T(8,128)(2,1)}), bf16[512,4096]{1,0:T(8,128)(2,1)}) %all-gather.5.cloned.1.call-update) | async-done | bytes 4194320 | tf_op jit(solution)/shard_map/all_gather | solution.py:26
  157.1 95.8 %all-reduce.2.cloned.1.call-done = f32[512,512]{1,0:T(8,128)} async-done(((f32[512,512]{1,0:T(8,128)}), f32[512,512]{1,0:T(8,128)}) %all-reduce.2.cloned.1.call-update) | async-done | bytes 1048592 | tf_op jit(solution)/shard_map/psum | solution.py:21
  252.9 13.6 %multiply_add_fusion = f32[1024,4096]{1,0:T(8,128)} fusion(f32[1024,4096]{1,0:T(8,128)} %param.7, bf16[512,4096]{1,0:T(8,128)(2,1)} %all-gather.5.cloned.1.call-done, bf16[512,1024]{1,0:T(8,128)(2,1)S(1)} %bitcast.11, f32[512,512]{1,0:T(8,128)} %all-reduce.2.cloned.1.call-done), kind=kOutput, calls=%fused_computation | convolution fusion | flops 4841275392 | bytes 39845888 | tf_op jit(solution)/shard_map/dot_general | solution.py:27
Async XLA Ops:
  6.5 99.4 %all-gather.3.cloned.1.call-start = ((), (), s32[]{:S(2)}) async-start(), calls=%async_computation.1 | async-start | bytes 8912896 | tf_op jit(solution)/shard_map/all_gather | solution.py:9
  7.3 149.8 %all-gather.5.cloned.1.call-start = ((), (), s32[]{:S(2)}) async-start(), calls=%async_computation.3 | async-start | bytes 4456448 | tf_op jit(solution)/shard_map/all_gather | solution.py:26
  11.3 106.4 %all-to-all-start = ((bf16[32,16,1024]{2,0,1:T(8,128)(2,1)}), bf16[32,16,1024]{2,0,1:T(8,128)(2,1)S(1)}, u32[]{:S(2)}, u32[]{:S(2)}) async-start(bf16[32,16,1024]{2,0,1:T(8,128)(2,1)} %bitcast.10), calls=%async_computation | async-start | bytes 2097152 | tf_op jit(solution)/shard_map/all_to_all | solution.py:8
  18.7 234.2 %all-reduce.2.cloned.1.call-start = ((), (), s32[]{:S(2)}) async-start(), calls=%async_computation.2 | async-start | bytes 2097152 | tf_op jit(solution)/shard_map/psum | solution.py:21
Sparse Core Ops, SparseCore 0:
  9.5 96.3 all-gather.2
  108.1 48.9 all-gather.4
  160.6 92.3 all-reduce.1
where the time goes:
time: 273 us
  waiting for transfers between devices  223 us (82%)
  matrix products  25.4 us (9%)
  between operations  13.1 us (5%)
  starting transfers between devices  7.5 us (3%)
  local copies, waits for them, and re-layouts  3.96 us (1%)
    psum x1, waiting for transfers between devices, per_device(): gram = (lax.psum(partial_value, 'row') * factor).astype(jnp.bfloat16)  95.8 us
    all_gather x1, waiting for transfers between devices, per_device(): whole = lax.all_gather(inputs, 'row', axis=0, tiled=True)  87.2 us
    all_gather x1, waiting for transfers between devices, per_device(): lax.all_gather(out_grads[:, :slab_width], 'row', axis=0, tiled=True)  39.4 us
    dot_general x1, matrix products, per_device(): update = jnp.dot(left, slab_all, preferred_element_type=jnp.float32)  13.6 us
    dot_general x1, matrix products, per_device(): lax.dot_general(proj_half, own_cols, (((0,), (1,)), ((), ())), preferred_...  11.8 us
    all_to_all x1, starting transfers between devices, per_device(): lax.all_to_all(out_grads, 'row', split_axis=1, concat_axis=0, tiled=True)  7.41 us
  transfers between devices with their start and end apart: 4, of which 3 were waited for; matrix products, arithmetic and copies ran while one was open for 6% of the time, Pallas kernels for 0%

commit v1 on v0

v1 whole, which is shorter than its diff:
```python
import functools

import jax
import jax.numpy as jnp
from jax import lax
from jax.experimental import pallas as pl
from jax.experimental.pallas import tpu as pltpu
from jax.sharding import PartitionSpec as P

UP, DOWN, SIDE, CORE = range(4)


def exchange_kernel(
    n, x_ref, f_ref, g_ref, gram_ref, slab_ref, cols_ref,
    xall, fv, gv, proj, part, out0, in0, out1, in1, out2, in2, final,
    local_sem, x_recv, x_send, s_recv, s_send, c_recv, c_send,
    r_recv, r_send, z2_recv, z2_send, z3_recv, z3_send,
):
    me = lax.axis_index("row")
    depth = n // 4
    z, y, c = me // 4, (me // 2) % 2, me % 2
    sh = x_ref.shape[0]
    tokens = n * sh
    slab = slab_ref.shape[1]
    width = cols_ref.shape[1]
    feat = f_ref.shape[0]

    def index(zz, yy, cc):
        return zz * 4 + yy * 2 + cc

    side, peer = index(z, 1 - y, c), index(z, y, 1 - c)

    def rows(start, size):
        return pl.ds(pl.multiple_of(start, size), size)

    load_f = pltpu.make_async_copy(f_ref, fv, local_sem.at[0])
    load_x = pltpu.make_async_copy(x_ref, xall.at[rows(me * sh, sh), :], local_sem.at[1])
    load_g = pltpu.make_async_copy(g_ref, gv, local_sem.at[2])
    load_x.start()
    load_g.start()
    load_f.start()

    barrier = pltpu.get_barrier_semaphore()
    for k in range(1, n):
        pl.semaphore_signal(
            barrier, inc=1, device_id={"row": (me + k) % n}, device_id_type=pl.DeviceIdType.MESH
        )
    pl.semaphore_wait(barrier, n - 1)

    def send(src, dst, send_sem, recv_sem, target):
        return pltpu.make_async_remote_copy(
            src_ref=src, dst_ref=dst, send_sem=send_sem, recv_sem=recv_sem,
            device_id={"row": target}, device_id_type=pl.DeviceIdType.MESH,
        )

    class Gather:
        def __init__(self, buf, recv, sems):
            self.buf, self.recv, self.sems = buf, recv, sems

        def copy(self, origin, kind, target, src=None):
            view = self.buf.at[rows(origin * sh, sh), :]
            return send(
                view if src is None else src, view,
                self.sems.at[kind, origin], self.recv.at[origin], target,
            )

        def arrived(self, origin):
            self.copy(origin, CORE, peer).wait_recv()

        def own(self, src):
            @pl.when(z + 1 < depth)
            def _():
                self.copy(me, UP, index(z + 1, y, c), src).start()

            @pl.when(z > 0)
            def _():
                self.copy(me, DOWN, index(z - 1, y, c), src).start()

            self.copy(me, SIDE, side, src).start()
            self.copy(me, CORE, peer, src).start()

        def column(self, k):
            @pl.when(z - k >= 0)
            def _():
                origin = index(z - k, y, c)
                self.arrived(origin)

                @pl.when(z + 1 < depth)
                def _():
                    self.copy(origin, UP, index(z + 1, y, c)).start()

                self.copy(origin, SIDE, side).start()
                self.copy(origin, CORE, peer).start()

            @pl.when(z + k < depth)
            def _():
                origin = index(z + k, y, c)
                self.arrived(origin)

                @pl.when(z > 0)
                def _():
                    self.copy(origin, DOWN, index(z - 1, y, c)).start()

                self.copy(origin, SIDE, side).start()
                self.copy(origin, CORE, peer).start()

        def across(self, plane):
            origin = index(plane, 1 - y, c)
            self.arrived(origin)
            self.copy(origin, CORE, peer).start()

        def whole(self, plane):
            self.arrived(index(plane, 0, 1 - c))
            self.arrived(index(plane, 1, 1 - c))

        def drain(self):
            for plane in range(depth):
                origin = index(plane, y, c)

                @pl.when((plane <= z) & (z + 1 < depth))
                def _():
                    self.copy(origin, UP, side).wait_send()

                @pl.when((plane >= z) & (z > 0))
                def _():
                    self.copy(origin, DOWN, side).wait_send()

                self.copy(origin, SIDE, side).wait_send()
                self.copy(origin, CORE, peer).wait_send()
                self.copy(index(plane, 1 - y, c), CORE, peer).wait_send()

    gx = Gather(xall, x_recv, x_send)
    gs = Gather(slab_ref, s_recv, s_send)
    gx.own(x_ref)

    flip = z >= (depth + 1) // 2
    zm = jnp.where(flip, depth - 1 - z, z)

    def plane_at(t):
        near = zm - (t + 1) // 2 if t % 2 else zm + t // 2
        p = jnp.where(t <= 2 * zm, near, t)
        return jnp.where(flip, depth - 1 - p, p)

    block = 4 * sh
    tile = min(256, feat)

    def project(plane):
        xs = rows(plane * block, block)

        @pl.loop(0, feat // tile)
        def _(j):
            fs = rows(j * tile, tile)
            proj[xs, fs] = lax.dot_general(
                xall[xs, :], fv[fs, :], (((1,), (1,)), ((), ())),
                preferred_element_type=jnp.float32,
            ).astype(jnp.bfloat16)

    def cols_copy(d, origin):
        return send(
            gv.at[:, rows(d * width, width)],
            cols_ref.at[rows(origin * sh, sh), :],
            c_send.at[d], c_recv.at[origin], d,
        )

    load_x.wait()
    load_g.wait()
    load_f.wait()
    own_slab = pltpu.make_async_copy(
        gv.at[:, pl.ds(0, slab)], slab_ref.at[rows(me * sh, sh), :], local_sem.at[3]
    )
    own_cols = pltpu.make_async_copy(
        gv.at[:, rows(me * width, width)], cols_ref.at[rows(me * sh, sh), :], local_sem.at[4]
    )
    own_slab.start()
    own_cols.start()

    for t in range(depth):
        if t > 0:
            gx.column(t)
        if t == depth - 1:
            gs.own(gv.at[:, pl.ds(0, slab)])
            for k in range(1, n):
                cols_copy((me + k) % n, me).start()
        plane = plane_at(t)
        gx.across(plane)
        gx.whole(plane)
        project(plane)

    own_features = rows(me * feat, feat)
    half, quarter = tokens // 2, tokens // 4

    def partial_rows(start, size):
        return lax.dot_general(
            proj[rows(start, size), :], xall[:, own_features], (((1,), (1,)), ((), ())),
            preferred_element_type=jnp.float32,
        )

    out0[...] = partial_rows((1 - c) * half, half).astype(jnp.bfloat16)
    core_sum = send(out0, in0, r_send.at[0], r_recv.at[0], peer)
    core_sum.start()
    part[...] = partial_rows(c * half, half)
    if depth > 1:
        gs.column(1)
    core_sum.wait_recv()
    gone, kept = rows((1 - y) * quarter, quarter), rows(y * quarter, quarter)
    out1[...] = (part[gone, :] + in0[gone, :].astype(jnp.float32)).astype(jnp.bfloat16)
    side_sum = send(out1, in1, r_send.at[1], r_recv.at[1], side)
    side_sum.start()
    part[kept, :] = part[kept, :] + in0[kept, :].astype(jnp.float32)
    if depth > 2:
        gs.column(2)
    side_sum.wait_recv()
    part[kept, :] = part[kept, :] + in1[...].astype(jnp.float32)
    out2[...] = part[kept, :].astype(jnp.bfloat16)

    def z_sum(k):
        zz = (z + k) % depth
        return send(
            out2.at[rows(zz * sh, sh), :], in2.at[k], z2_send.at[k], z2_recv.at[k], index(zz, y, c)
        )

    for k in range(1, depth):
        z_sum(k).start()
    total = part[rows(y * quarter + z * sh, sh), :]
    for k in range(1, depth):
        z_sum(k).wait_recv()
        total = total + in2[k].astype(jnp.float32)
    scale = float(n * feat) ** (-0.5)
    base = c * half + y * quarter
    mine = rows(base + z * sh, sh)
    final[mine, :] = (total * scale).astype(jnp.bfloat16)

    def z_spread(k):
        zz = (z + k) % depth
        return send(
            final.at[mine, :], final.at[mine, :], z3_send.at[k], z3_recv.at[k], index(zz, y, c)
        )

    for k in range(1, depth):
        z_spread(k).start()
    for k in range(3, depth):
        gs.column(k)
    for k in range(1, depth):
        z_spread(k).wait_recv()
    view = final.at[rows(base, quarter), :]
    side_spread = send(view, view, r_send.at[2], r_recv.at[2], side)
    side_spread.start()
    side_spread.wait_recv()
    view = final.at[rows(c * half, half), :]
    core_spread = send(view, view, r_send.at[3], r_recv.at[3], peer)
    core_spread.start()
    for t in range(depth):
        gs.across(plane_at(t))
    core_spread.wait_recv()
    gram_ref[...] = final[...]
    for t in range(depth):
        gs.whole(plane_at(t))
    for k in range(1, n):
        cols_copy(me, (me + k) % n).wait_recv()

    gx.drain()
    gs.drain()
    for k in range(1, n):
        cols_copy((me + k) % n, me).wait_send()
    for copy in (core_sum, side_sum, side_spread, core_spread):
        copy.wait_send()
    for k in range(1, depth):
        z_sum(k).wait_send()
        z_spread(k).wait_send()
    own_slab.wait()
    own_cols.wait()


def exchange(n, x, f, g, slab):
    sh, din = x.shape
    feat = f.shape[0]
    tokens, depth = n * sh, n // 4
    width = g.shape[1] // n
    half, quarter = tokens // 2, tokens // 4
    bf, dma = jnp.bfloat16, pltpu.SemaphoreType.DMA
    anyspace = pl.BlockSpec(memory_space=pl.ANY)
    return pl.pallas_call(
        functools.partial(exchange_kernel, n),
        out_shape=(
            jax.ShapeDtypeStruct((tokens, tokens), bf),
            jax.ShapeDtypeStruct((tokens, slab), bf),
            jax.ShapeDtypeStruct((tokens, width), bf),
        ),
        in_specs=[anyspace] * 3,
        out_specs=(pl.BlockSpec(memory_space=pltpu.VMEM), anyspace, anyspace),
        scratch_shapes=[
            pltpu.VMEM((tokens, din), bf),
            pltpu.VMEM(f.shape, bf),
            pltpu.VMEM(g.shape, bf),
            pltpu.VMEM((tokens, feat), bf),
            pltpu.VMEM((half, tokens), jnp.float32),
            pltpu.VMEM((half, tokens), bf),
            pltpu.VMEM((half, tokens), bf),
            pltpu.VMEM((quarter, tokens), bf),
            pltpu.VMEM((quarter, tokens), bf),
            pltpu.VMEM((quarter, tokens), bf),
            pltpu.VMEM((depth, sh, tokens), bf),
            pltpu.VMEM((tokens, tokens), bf),
            dma((5,)), dma((n,)), dma((4, n)), dma((n,)), dma((4, n)),
            dma((n,)), dma((n,)), dma((4,)), dma((4,)),
            dma((depth,)), dma((depth,)), dma((depth,)), dma((depth,)),
        ],
        compiler_params=pltpu.CompilerParams(
            collective_id=0, has_side_effects=True, vmem_limit_bytes=60 * 1024 * 1024
        ),
    )(x, f, g)


def per_device(n, inputs, input_factor, out_grads, output_factor):
    slab_width = output_factor.shape[1]
    gram, slab_all, grad_cols = exchange(n, inputs, input_factor, out_grads, slab_width)
    left = lax.dot_general(
        grad_cols, gram, (((0,), (0,)), ((), ())), preferred_element_type=jnp.float32
    ).astype(jnp.bfloat16)
    update = jnp.dot(left, slab_all, preferred_element_type=jnp.float32)
    return output_factor + update * (1.0 / gram.shape[0])


def solution(mesh):
    spec = P(("groups", "row"), None)
    return jax.shard_map(
        functools.partial(per_device, mesh.shape["row"]),
        mesh=mesh, in_specs=(spec,) * 4, out_specs=spec, check_vma=False,
    )
```

time: 273 us -> 136 us (0.50)
  waiting for transfers between devices: 223 us -> 0 us
  Pallas kernels: 0 us -> 122 us
  between operations: 13.1 us -> 0.01 us
  matrix products: 25.4 us -> 13.8 us
  starting transfers between devices: 7.5 us -> 0 us
  local copies, waits for them, and re-layouts: 3.96 us -> 0 us
    all_gather x2 -> x0, waiting for transfers between devices: 127 us -> none  [the longest x1 87.2 us: per_device(): whole = lax.all_gather(inputs, 'row', axis=0, tiled=True)]
    pallas_call x0 -> x1, Pallas kernels: none -> 122 us  [exchange(): pl.pallas_call(functools.partial(exchange_kernel, n), out_shape=(jax.Shap...]
    psum x1 -> x0, waiting for transfers between devices: 95.8 us -> none  [per_device(): gram = (lax.psum(partial_value, 'row') * factor).astype(jnp.bfloat16)]
    dot_general x1 -> x0, matrix products: 11.8 us -> none  [per_device(): lax.dot_general(proj_half, own_cols, (((0,), (1,)), ((), ())), preferred_...]
    all_to_all x1 -> x0, starting transfers between devices: 7.41 us -> none  [per_device(): lax.all_to_all(out_grads, 'row', split_axis=1, concat_axis=0, tiled=True)]
  transfers between devices with their start and end apart: 4 -> 0, of which waited for: 3 -> 0; matrix products, arithmetic and copies ran while one was open for 6% -> 0% of each run, Pallas kernels for 0% -> 0%
where the time goes in v1:
time: 136 us; the launch traced here: 135 us
  Pallas kernels  122 us (90%)
  matrix products  13.8 us (10%)
    pallas_call x1, Pallas kernels, exchange(): pl.pallas_call(functools.partial(exchange_kernel, n), out_shape=(jax.Shap...  122 us
    dot_general x1, matrix products, per_device(): update = jnp.dot(left, slab_all, preferred_element_type=jnp.float32)  13.8 us

profile of v1, /device:TPU:0, one launch (start us, length us, event | category | flops | bytes accessed | tf_op | source)
XLA Modules:
  0.0 135.4 jit_solution(16472038581354445665)
XLA Ops:
  0.0 121.6 %shard_map.46 = (bf16[512,512]{1,0:T(8,128)(2,1)}, bf16[512,4096]{1,0:T(8,128)(2,1)}, bf16[512,1024]{1,0:T(8,128)(2,1)}) custom-call(bf16[32,8192]{1,0:T(8,128)(2,1)} %x_ref.1, bf16[512,8192]{1,0:T(8,128)(2,1)} %f_ref.1, bf16[32,16384]{1,0:T(8,128)(2,1)} %g_ref.1), custom_call_target="tpu_custom_call" | custom-call | tf_op jit(solution)/shard_map/pallas_call | solution.py:282
  121.6 13.8 %multiply_add_fusion = f32[1024,4096]{1,0:T(8,128)} fusion(f32[1024,4096]{1,0:T(8,128)} %param.7, bf16[512,4096]{1,0:T(8,128)(2,1)} %get-tuple-element.10, bf16[512,1024]{1,0:T(8,128)(2,1)} %get-tuple-element.8, bf16[512,512]{1,0:T(8,128)(2,1)} %get-tuple-element.9), kind=kOutput, calls=%fused_computation | convolution fusion | flops 4840751104 | bytes 39321600 | tf_op jit(solution)/shard_map/dot_general | solution.py:320

commit v2 on v1

--- a/solution.py
+++ b/solution.py
@@ -12,7 +12,7 @@
 
 def exchange_kernel(
     n, x_ref, f_ref, g_ref, gram_ref, slab_ref, cols_ref,
-    xall, fv, gv, proj, part, out0, in0, out1, in1, out2, in2, final,
+    xall, fv, gv, proj, proj_low, part, out0, in0, out1, in1, out2, in2, final,
     local_sem, x_recv, x_send, s_recv, s_send, c_recv, c_send,
     r_recv, r_send, z2_recv, z2_send, z3_recv, z3_send,
 ):
@@ -53,84 +53,126 @@
             device_id={"row": target}, device_id_type=pl.DeviceIdType.MESH,
         )
 
+    chips = n // 2
+    chip = z * 2 + y
+    window = min(chips, chips // 2 + 1)
+    union = min(chips, window + 1)
+
     class Gather:
-        def __init__(self, buf, recv, sems):
-            self.buf, self.recv, self.sems = buf, recv, sems
-
-        def copy(self, origin, kind, target, src=None):
-            view = self.buf.at[rows(origin * sh, sh), :]
+        def __init__(self, buf, recv, sems, pieces):
+            self.buf, self.recv, self.sems, self.pieces = buf, recv, sems, pieces
+            self.width = buf.shape[1] // pieces
+            self.near = window if pieces > 1 else 1
+            self.end = union if pieces > 1 else 1
+
+        def copy(self, origin, kind, target, first, count, src=None):
+            cols = pl.ds(pl.multiple_of(first * self.width, self.width), count * self.width)
+            view = self.buf.at[rows(origin * sh, sh), cols]
             return send(
-                view if src is None else src, view,
+                view if src is None else src.at[:, cols], view,
                 self.sems.at[kind, origin], self.recv.at[origin], target,
             )
 
-        def arrived(self, origin):
-            self.copy(origin, CORE, peer).wait_recv()
+        def start(self, origin, kind, target, first, count, src=None):
+            if self.pieces == 1:
+                self.copy(origin, kind, target, 0, 1, src).start()
+                return
+
+            @pl.loop(0, count)
+            def _(k):
+                self.copy(origin, kind, target, (first + k) % self.pieces, 1, src).start()
+
+        def along(self, origin, kind, src=None):
+            to = z + 1 if kind == UP else z - 1
+            last = (to == depth - 1) | (to == 0)
+            count = jnp.where(last, self.end, self.pieces)
+            self.start(origin, kind, index(to, y, c), to * 2, count, src)
+
+        def near_by(self, origin, src=None):
+            self.start(origin, SIDE, side, z * 2 + 1 - y, self.near, src)
+            self.start(origin, CORE, peer, chip, self.near, src)
+
+        def arrived(self, origin, count):
+            self.copy(origin, CORE, peer, 0, count).wait_recv()
 
         def own(self, src):
             @pl.when(z + 1 < depth)
             def _():
-                self.copy(me, UP, index(z + 1, y, c), src).start()
+                self.along(me, UP, src)
 
             @pl.when(z > 0)
             def _():
-                self.copy(me, DOWN, index(z - 1, y, c), src).start()
-
-            self.copy(me, SIDE, side, src).start()
-            self.copy(me, CORE, peer, src).start()
+                self.along(me, DOWN, src)
+
+            self.near_by(me, src)
 
         def column(self, k):
+            def came(origin):
+                last = (z == depth - 1) | (z == 0)
+
+                @pl.when(last)
+                def _():
+                    self.arrived(origin, self.end)
+
+                @pl.when(jnp.logical_not(last))
+                def _():
+                    self.arrived(origin, self.pieces)
+
             @pl.when(z - k >= 0)
             def _():
                 origin = index(z - k, y, c)
-                self.arrived(origin)
+                came(origin)
 
                 @pl.when(z + 1 < depth)
                 def _():
-                    self.copy(origin, UP, index(z + 1, y, c)).start()
-
-                self.copy(origin, SIDE, side).start()
-                self.copy(origin, CORE, peer).start()
+                    self.along(origin, UP)
+
+                self.near_by(origin)
 
             @pl.when(z + k < depth)
             def _():
                 origin = index(z + k, y, c)
-                self.arrived(origin)
+                came(origin)
 
                 @pl.when(z > 0)
                 def _():
-                    self.copy(origin, DOWN, index(z - 1, y, c)).start()
-
-                self.copy(origin, SIDE, side).start()
-                self.copy(origin, CORE, peer).start()
+                    self.along(origin, DOWN)
+
+                self.near_by(origin)
 
         def across(self, plane):
             origin = index(plane, 1 - y, c)
-            self.arrived(origin)
-            self.copy(origin, CORE, peer).start()
+            self.arrived(origin, self.near)
+            self.start(origin, CORE, peer, chip, self.near)
 
         def whole(self, plane):
-            self.arrived(index(plane, 0, 1 - c))
-            self.arrived(index(plane, 1, 1 - c))
+            self.arrived(index(plane, 0, 1 - c), self.near)
+            self.arrived(index(plane, 1, 1 - c), self.near)
 
         def drain(self):
+            def sent(origin, kind, count):
+                self.copy(origin, kind, peer, 0, count).wait_send()
+
             for plane in range(depth):
                 origin = index(plane, y, c)
-
-                @pl.when((plane <= z) & (z + 1 < depth))
-                def _():
-                    self.copy(origin, UP, side).wait_send()
-
-                @pl.when((plane >= z) & (z > 0))
-                def _():
-                    self.copy(origin, DOWN, side).wait_send()
-
-                self.copy(origin, SIDE, side).wait_send()
-                self.copy(origin, CORE, peer).wait_send()
-                self.copy(index(plane, 1 - y, c), CORE, peer).wait_send()
-
-    gx = Gather(xall, x_recv, x_send)
-    gs = Gather(slab_ref, s_recv, s_send)
+                for kind, edge, gate in (
+                    (UP, z + 1 == depth - 1, (plane <= z) & (z + 1 < depth)),
+                    (DOWN, z - 1 == 0, (plane >= z) & (z > 0)),
+                ):
+                    @pl.when(gate & edge)
+                    def _():
+                        sent(origin, kind, self.end)
+
+                    @pl.when(gate & jnp.logical_not(edge))
+                    def _():
+                        sent(origin, kind, self.pieces)
+
+                sent(origin, SIDE, self.near)
+                sent(origin, CORE, self.near)
+                sent(index(plane, 1 - y, c), CORE, self.near)
+
+    gx = Gather(xall, x_recv, x_send, chips)
+    gs = Gather(slab_ref, s_recv, s_send, 1)
     gx.own(x_ref)
 
     flip = z >= (depth + 1) // 2
@@ -150,10 +192,21 @@
         @pl.loop(0, feat // tile)
         def _(j):
             fs = rows(j * tile, tile)
-            proj[xs, fs] = lax.dot_general(
-                xall[xs, :], fv[fs, :], (((1,), (1,)), ((), ())),
-                preferred_element_type=jnp.float32,
-            ).astype(jnp.bfloat16)
+            edge, inner = jnp.zeros((block, tile), jnp.float32), jnp.zeros((block, tile), jnp.float32)
+            for k in range(window):
+                cs = rows((chip + k) % chips * (2 * feat), 2 * feat)
+                term = lax.dot_general(
+                    xall[xs, cs], fv[fs, cs], (((1,), (1,)), ((), ())),
+                    preferred_element_type=jnp.float32,
+                )
+                if k == 0 or 2 * k == chips:
+                    edge = edge + term
+                else:
+                    inner = inner + term
+            value = inner + 0.5 * edge
+            high = value.astype(jnp.bfloat16)
+            proj[xs, fs] = high
+            proj_low[xs, fs] = (value - high.astype(jnp.float32)).astype(jnp.bfloat16)
 
     def cols_copy(d, origin):
         return send(
@@ -190,12 +243,16 @@
     half, quarter = tokens // 2, tokens // 4
 
     def partial_rows(start, size):
-        return lax.dot_general(
-            proj[rows(start, size), :], xall[:, own_features], (((1,), (1,)), ((), ())),
-            preferred_element_type=jnp.float32,
-        )
-
-    out0[...] = partial_rows((1 - c) * half, half).astype(jnp.bfloat16)
+        some = rows(start, size)
+        total = jnp.zeros((size, tokens), jnp.float32)
+        for piece in (proj, proj_low):
+            for left, right in ((piece[some, :], xall[:, own_features]), (xall[some, own_features], piece[...])):
+                total = total + lax.dot_general(
+                    left, right, (((1,), (1,)), ((), ())), preferred_element_type=jnp.float32
+                )
+        return total
+
+    out0[...] = partial_rows((1 - c) * half, half)
     core_sum = send(out0, in0, r_send.at[0], r_recv.at[0], peer)
     core_sum.start()
     part[...] = partial_rows(c * half, half)
@@ -203,10 +260,10 @@
         gs.column(1)
     core_sum.wait_recv()
     gone, kept = rows((1 - y) * quarter, quarter), rows(y * quarter, quarter)
-    out1[...] = (part[gone, :] + in0[gone, :].astype(jnp.float32)).astype(jnp.bfloat16)
+    out1[...] = (part[gone, :] + in0[gone, :]).astype(jnp.bfloat16)
     side_sum = send(out1, in1, r_send.at[1], r_recv.at[1], side)
     side_sum.start()
-    part[kept, :] = part[kept, :] + in0[kept, :].astype(jnp.float32)
+    part[kept, :] = part[kept, :] + in0[kept, :]
     if depth > 2:
         gs.column(2)
     side_sum.wait_recv()
@@ -293,9 +350,10 @@
             pltpu.VMEM(f.shape, bf),
             pltpu.VMEM(g.shape, bf),
             pltpu.VMEM((tokens, feat), bf),
+            pltpu.VMEM((tokens, feat), bf),
             pltpu.VMEM((half, tokens), jnp.float32),
-            pltpu.VMEM((half, tokens), bf),
-            pltpu.VMEM((half, tokens), bf),
+            pltpu.VMEM((half, tokens), jnp.float32),
+            pltpu.VMEM((half, tokens), jnp.float32),
             pltpu.VMEM((quarter, tokens), bf),
             pltpu.VMEM((quarter, tokens), bf),
             pltpu.VMEM((quarter, tokens), bf),

time: 136 us -> 115 us (0.85)
  Pallas kernels: 122 us -> 101 us
    pallas_call x1, Pallas kernels: 122 us -> 101 us  [exchange(): pl.pallas_call(functools.partial(exchange_kernel, n), out_shape=(jax.Shap...]
where the time goes in v2:
time: 115 us
  Pallas kernels  101 us (88%)
  matrix products  13.8 us (12%)
    pallas_call x1, Pallas kernels, exchange(): pl.pallas_call(functools.partial(exchange_kernel, n), out_shape=(jax.Shap...  101 us
    dot_general x1, matrix products, per_device(): update = jnp.dot(left, slab_all, preferred_element_type=jnp.float32)  13.8 us

profile of v2, /device:TPU:0, one launch (start us, length us, event | category | flops | bytes accessed | tf_op | source)
XLA Modules:
  0.0 114.9 jit_solution(6783831145602303114)
XLA Ops:
  0.0 101.1 %shard_map.46 = (bf16[512,512]{1,0:T(8,128)(2,1)}, bf16[512,4096]{1,0:T(8,128)(2,1)}, bf16[512,1024]{1,0:T(8,128)(2,1)}) custom-call(bf16[32,8192]{1,0:T(8,128)(2,1)} %x_ref.1, bf16[512,8192]{1,0:T(8,128)(2,1)} %f_ref.1, bf16[32,16384]{1,0:T(8,128)(2,1)} %g_ref.1), custom_call_target="tpu_custom_call" | custom-call | tf_op jit(solution)/shard_map/pallas_call | solution.py:339
  101.1 13.8 %multiply_add_fusion = f32[1024,4096]{1,0:T(8,128)} fusion(f32[1024,4096]{1,0:T(8,128)} %param.7, bf16[512,4096]{1,0:T(8,128)(2,1)} %get-tuple-element.10, bf16[512,1024]{1,0:T(8,128)(2,1)} %get-tuple-element.8, bf16[512,512]{1,0:T(8,128)(2,1)} %get-tuple-element.9), kind=kOutput, calls=%fused_computation | convolution fusion | flops 4840751104 | bytes 39321600 | tf_op jit(solution)/shard_map/dot_general | solution.py:378

commit v3 on v2

--- a/solution.py
+++ b/solution.py
@@ -227,13 +227,23 @@
     own_slab.start()
     own_cols.start()
 
+    def send_cols(part, parts):
+        for k in range(1, n):
+            if k * parts // n == part:
+                cols_copy((me + k * 5) % n if n % 5 else (me + k) % n, me).start()
+
+    SLAB_AT = depth - 2
+    COLS_AT = -1
+    done = depth - 1 - SLAB_AT
     for t in range(depth):
         if t > 0:
             gx.column(t)
-        if t == depth - 1:
+        if t == SLAB_AT:
             gs.own(gv.at[:, pl.ds(0, slab)])
-            for k in range(1, n):
-                cols_copy((me + k) % n, me).start()
+        if t > SLAB_AT:
+            gs.column(t - SLAB_AT)
+        if t == COLS_AT:
+            send_cols(0, 1)
         plane = plane_at(t)
         gx.across(plane)
         gx.whole(plane)
@@ -256,16 +266,20 @@
     core_sum = send(out0, in0, r_send.at[0], r_recv.at[0], peer)
     core_sum.start()
     part[...] = partial_rows(c * half, half)
-    if depth > 1:
-        gs.column(1)
+    if COLS_AT < 0:
+        send_cols(0, 4)
+    if done + 1 < depth:
+        gs.column(done + 1)
     core_sum.wait_recv()
     gone, kept = rows((1 - y) * quarter, quarter), rows(y * quarter, quarter)
     out1[...] = (part[gone, :] + in0[gone, :]).astype(jnp.bfloat16)
     side_sum = send(out1, in1, r_send.at[1], r_recv.at[1], side)
     side_sum.start()
     part[kept, :] = part[kept, :] + in0[kept, :]
-    if depth > 2:
-        gs.column(2)
+    if COLS_AT < 0:
+        send_cols(1, 4)
+    for k in range(done + 2, depth):
+        gs.column(k)
     side_sum.wait_recv()
     part[kept, :] = part[kept, :] + in1[...].astype(jnp.float32)
     out2[...] = part[kept, :].astype(jnp.bfloat16)
@@ -278,6 +292,10 @@
 
     for k in range(1, depth):
         z_sum(k).start()
+    if COLS_AT < 0:
+        send_cols(2, 4)
+    for t in range(depth // 2):
+        gs.across(plane_at(t))
     total = part[rows(y * quarter + z * sh, sh), :]
     for k in range(1, depth):
         z_sum(k).wait_recv()
@@ -295,8 +313,10 @@
 
     for k in range(1, depth):
         z_spread(k).start()
-    for k in range(3, depth):
-        gs.column(k)
+    if COLS_AT < 0:
+        send_cols(3, 4)
+    for t in range(depth // 2, depth):
+        gs.across(plane_at(t))
     for k in range(1, depth):
         z_spread(k).wait_recv()
     view = final.at[rows(base, quarter), :]
@@ -306,8 +326,6 @@
     view = final.at[rows(c * half, half), :]
     core_spread = send(view, view, r_send.at[3], r_recv.at[3], peer)
     core_spread.start()
-    for t in range(depth):
-        gs.across(plane_at(t))
     core_spread.wait_recv()
     gram_ref[...] = final[...]
     for t in range(depth):

time: 115 us -> 117 us (1.017)
  Pallas kernels: 101 us -> 103 us
    pallas_call x1, Pallas kernels: 101 us -> 103 us  [exchange(): pl.pallas_call(functools.partial(exchange_kernel, n), out_shape=(jax.Shap...]
where the time goes in v3:
time: 117 us
  Pallas kernels  103 us (88%)
  matrix products  13.8 us (12%)
    pallas_call x1, Pallas kernels, exchange(): pl.pallas_call(functools.partial(exchange_kernel, n), out_shape=(jax.Shap...  103 us
    dot_general x1, matrix products, per_device(): update = jnp.dot(left, slab_all, preferred_element_type=jnp.float32)  13.8 us

profile of v3, /device:TPU:0, one launch (start us, length us, event | category | flops | bytes accessed | tf_op | source)
XLA Modules:
  0.0 116.5 jit_solution(2612062306586122279)
XLA Ops:
  0.0 102.7 %shard_map.46 = (bf16[512,512]{1,0:T(8,128)(2,1)}, bf16[512,4096]{1,0:T(8,128)(2,1)}, bf16[512,1024]{1,0:T(8,128)(2,1)}) custom-call(bf16[32,8192]{1,0:T(8,128)(2,1)} %x_ref.1, bf16[512,8192]{1,0:T(8,128)(2,1)} %f_ref.1, bf16[32,16384]{1,0:T(8,128)(2,1)} %g_ref.1), custom_call_target="tpu_custom_call" | custom-call | tf_op jit(solution)/shard_map/pallas_call | solution.py:357
  102.7 13.8 %multiply_add_fusion = f32[1024,4096]{1,0:T(8,128)} fusion(f32[1024,4096]{1,0:T(8,128)} %param.7, bf16[512,4096]{1,0:T(8,128)(2,1)} %get-tuple-element.10, bf16[512,1024]{1,0:T(8,128)(2,1)} %get-tuple-element.8, bf16[512,512]{1,0:T(8,128)(2,1)} %get-tuple-element.9), kind=kOutput, calls=%fused_computation | convolution fusion | flops 4840751104 | bytes 39321600 | tf_op jit(solution)/shard_map/dot_general | solution.py:396

commit v4 on v3

--- a/solution.py
+++ b/solution.py
@@ -233,7 +233,7 @@
                 cols_copy((me + k * 5) % n if n % 5 else (me + k) % n, me).start()
 
     SLAB_AT = depth - 2
-    COLS_AT = -1
+    COLS_AT = depth - 1
     done = depth - 1 - SLAB_AT
     for t in range(depth):
         if t > 0:

time: 117 us -> 113 us (0.966)
  Pallas kernels: 103 us -> 98.9 us
    pallas_call x1, Pallas kernels: 103 us -> 98.9 us  [exchange(): pl.pallas_call(functools.partial(exchange_kernel, n), out_shape=(jax.Shap...]
where the time goes in v4:
time: 113 us
  Pallas kernels  98.9 us (88%)
  matrix products  13.8 us (12%)
    pallas_call x1, Pallas kernels, exchange(): pl.pallas_call(functools.partial(exchange_kernel, n), out_shape=(jax.Shap...  98.9 us
    dot_general x1, matrix products, per_device(): update = jnp.dot(left, slab_all, preferred_element_type=jnp.float32)  13.8 us

profile of v4, /device:TPU:0, one launch (start us, length us, event | category | flops | bytes accessed | tf_op | source)
XLA Modules:
  0.0 112.7 jit_solution(4149118801871801246)
XLA Ops:
  0.0 98.9 %shard_map.46 = (bf16[512,512]{1,0:T(8,128)(2,1)}, bf16[512,4096]{1,0:T(8,128)(2,1)}, bf16[512,1024]{1,0:T(8,128)(2,1)}) custom-call(bf16[32,8192]{1,0:T(8,128)(2,1)} %x_ref.1, bf16[512,8192]{1,0:T(8,128)(2,1)} %f_ref.1, bf16[32,16384]{1,0:T(8,128)(2,1)} %g_ref.1), custom_call_target="tpu_custom_call" | custom-call | tf_op jit(solution)/shard_map/pallas_call | solution.py:357
  98.9 13.8 %multiply_add_fusion = f32[1024,4096]{1,0:T(8,128)} fusion(f32[1024,4096]{1,0:T(8,128)} %param.7, bf16[512,4096]{1,0:T(8,128)(2,1)} %get-tuple-element.10, bf16[512,1024]{1,0:T(8,128)(2,1)} %get-tuple-element.8, bf16[512,512]{1,0:T(8,128)(2,1)} %get-tuple-element.9), kind=kOutput, calls=%fused_computation | convolution fusion | flops 4840751104 | bytes 39321600 | tf_op jit(solution)/shard_map/dot_general | solution.py:396
